TPU v7x, 32 devices: a whole 2x2x4 slice. The times are simulated.
32 devices in a mesh: region: 2 (over y), member: 8 (over z, core), space: 2 (over x).
Axes of the slice: x: 2, y: 2, z: 4, core: 2. Of those that a mesh axis runs over, the one named last changes fastest.
Arguments:
- prior_trials: bfloat16 [80, 1536, 256], P('member', ('region', 'space')), parts along dimension 1, may hold values from -6 to 6
- prior_at_sensors: bfloat16 [80, 1536], P('member', ('region', 'space')), parts along dimension 1, may hold values from -6 to 6
- sensor_readings: bfloat16 [1536], P(('region', 'space')), parts along dimension 0, may hold values from -8 to 8
- sensor_noise_spread: bfloat16 [1536], P(('region', 'space')), parts along dimension 0, may hold values from 1 to 10
- nearby_readings: int32 [1536, 128], P(('region', 'space')), parts along dimension 0, may hold values from 0 to 1023, as said below
- subarea_cutoff_level: int32 [1536], P(('region', 'space')), parts along dimension 0, may hold values from 0 to 3
Outputs:
- analysis: bfloat16 [80, 1536, 256], P('member', ('region', 'space')), parts along dimension 1
There are 2 independent parts, one for each index of `region`. A program takes and returns all parts, laid end to end along the dimension named above; each array names one. Nothing has to cross between parts.
Inputs may be any that keep to these rules, and one draw needn't show every extreme that they name: `nearby_readings`: row c lists 128 distinct observations whose region-wide index o lies within (subarea_cutoff_level[c] + 2) * 64 of c and inside the region.
All inputs are finite; a program needn't handle non-finite values. Where the computation divides by a largest or mean magnitude, that divisor is 1e-20 or more.
Results may differ from a plain program's by a relative error of at most 0.0053.
Values may be sent and summed in bfloat16 or wider, within the bound.
A program may use at most 64 MiB of HBM per device.

v0:
```python
import jax
import jax.numpy as jnp
from jax import lax
from jax.sharding import PartitionSpec as P

NS_STEPS = 4


def padded(value, sides, width):
    for axis, dim in sides:
        count, length = (lax.axis_size(axis), value.shape[dim])
        up = [(i, (i + 1) % count) for i in range(count - 1)]
        down = [(j, i) for i, j in up]
        last = lax.slice_in_dim(value, length - width, length, axis=dim)
        leading = lax.slice_in_dim(value, 0, width, axis=dim)
        before = lax.ppermute(last, axis, up)
        after = lax.ppermute(leading, axis, down)
        value = jnp.concatenate([before, value, after], axis=dim)
    return value


def prepare(picked, trial_lines, offsets, tier_ids, obs_count):
    observ = picked[:trial_lines]
    ens_mean = jnp.mean(observ, axis=0)
    anomaly = observ - ens_mean
    innovation = picked[trial_lines] - ens_mean
    radius = (tier_ids.astype(jnp.float32) + 2.0) * (0.5 * obs_count)
    distance = jnp.abs(offsets).astype(jnp.float32) / radius[:, None]
    weight = jnp.exp(-2.0 * distance * distance) / picked[trial_lines + 1]
    return (anomaly, innovation, weight)


def spread_terms(anomaly, innovation, weight, trial_lines):
    fit_sum = jnp.sum(weight * innovation * innovation)
    spread = jnp.sum(weight * jnp.sum(anomaly * anomaly, axis=0)) / (trial_lines - 1.0)
    return (fit_sum, spread)


def transform(anomaly, innovation, weight, inflation, trial_lines, sweeps):
    exact = lax.Precision.HIGHEST
    weighted = anomaly * weight[None]
    gram = jnp.einsum("ank,bnk->abn", weighted, anomaly, precision=exact)
    identity = jnp.eye(trial_lines, dtype=jnp.float32)[:, :, None]
    matrix = gram + (trial_lines - 1.0) / inflation * identity
    row_bound = jnp.max(jnp.sum(jnp.abs(matrix), axis=1), axis=0)
    root_iter = matrix / row_bound
    inverse = jnp.broadcast_to(identity, matrix.shape)
    for repeat in range(sweeps):
        factor = 1.5 * identity - 0.5 * jnp.einsum(
            "abn,bcn->acn", inverse, root_iter, precision=exact
        )
        root_iter = jnp.einsum("abn,bcn->acn", root_iter, factor, precision=exact)
        inverse = jnp.einsum("abn,bcn->acn", factor, inverse, precision=exact)
    inv_root = inverse / jnp.sqrt(row_bound)
    target = jnp.sum(weighted * innovation[None], axis=2)
    half_gain = jnp.einsum("abn,bn->an", inv_root, target, precision=exact)
    mean_gain = jnp.einsum("abn,bn->an", inv_root, half_gain, precision=exact)
    weights_full = jnp.sqrt(trial_lines - 1.0) * inv_root + mean_gain[:, None, :]
    centred = weights_full - jnp.mean(weights_full, axis=0, keepdims=True) + 1.0 / trial_lines
    return centred.astype(jnp.bfloat16)


def select_domains(window, trial_lines, obs_lists, col_ids, tier_ids, halo_cells):
    row_count = window.shape[0]
    dom_count, obs_count = obs_lists.shape
    picked = jnp.take(window, obs_lists.reshape(-1), axis=1).reshape(
        row_count, dom_count, obs_count
    )
    picked = picked.astype(jnp.float32)
    offsets = obs_lists - (col_ids + halo_cells)[:, None]
    return prepare(picked, trial_lines, offsets, tier_ids, obs_count)


def per_device(
    prior_trials,
    prior_at_sensors,
    sensor_readings,
    sensor_noise_spread,
    nearby_readings,
    subarea_cutoff_level,
):
    patch_cells = prior_trials.shape[1]
    obs_count = nearby_readings.shape[1]
    halo_cells = 5 * obs_count // 2
    groups = lax.axis_size("member")
    domains = patch_cells // groups
    obs_rows = jnp.stack([sensor_readings, sensor_noise_spread], axis=0)
    gathered = lax.all_gather(prior_at_sensors, "member", axis=0, tiled=True)
    window = padded(jnp.concatenate([gathered, obs_rows], axis=0), (("space", 1),), halo_cells)
    trial_lines = window.shape[0] - 2
    first_col = lax.axis_index("member") * domains
    own_lists = lax.dynamic_slice_in_dim(nearby_readings, first_col, domains, 0)
    own_tiers = lax.dynamic_slice_in_dim(subarea_cutoff_level, first_col, domains, 0)
    own_columns = first_col + jnp.arange(domains, dtype=jnp.int32)
    anomaly, innovation, weight = select_domains(
        window, trial_lines, own_lists, own_columns, own_tiers, halo_cells
    )
    fit_sum, spread = spread_terms(anomaly, innovation, weight, trial_lines)
    fit_sum, spread = lax.psum((fit_sum, spread), ("member", "space"))
    inflation = fit_sum / spread
    trans_w = transform(anomaly, innovation, weight, inflation, trial_lines, NS_STEPS)
    incoming_pieces = lax.all_to_all(
        prior_trials, "member", split_axis=1, concat_axis=0, tiled=True
    )
    updated = jnp.einsum(
        "inc,ijn->jnc", incoming_pieces, trans_w, preferred_element_type=jnp.float32
    ).astype(jnp.bfloat16)
    return lax.all_to_all(updated, "member", split_axis=0, concat_axis=1, tiled=True)


def solution(mesh):
    return jax.shard_map(
        per_device,
        mesh=mesh,
        in_specs=(
            P("member", ("region", "space"), None),
            P("member", ("region", "space")),
            P(("region", "space")),
            P(("region", "space")),
            P(("region", "space"), None),
            P(("region", "space")),
        ),
        out_specs=P("member", ("region", "space"), None),
        check_vma=False,
    )
```

profile of v0, /device:TPU:0, one launch (start us, length us, event | category | flops | bytes accessed | tf_op | source)
XLA Modules:
  0.0 223.0 jit_solution(4702585472627936783)
XLA Ops:
  0.0 15.8 %all-gather = bf16[8,10,384]{2,1,0:T(8,128)(2,1)S(1)} all-gather(bf16[1,10,384]{2,1,0:T(8,128)(2,1)} %bitcast.124), channel_id=1, replica_groups=mesh['region'=2,'member'=8,'space'=2] {'member'}, dimensions={0}, use_global_device_ids=true | all-gather | bytes 69120 | tf_op jit(solution)/shard_map/all_gather | solution.py:88
  15.9 0.1 copy.66
  16.0 0.8 stack.8
  16.8 0.8 stack.9
  17.6 0.1 pad_maximum_fusion.1
  17.7 3.4 %collective-permute-start = (bf16[82,320]{0,1:T(8,128)(2,1)S(1)}, bf16[82,320]{0,1:T(8,128)(2,1)S(1)}, u32[]{:S(2)}, u32[]{:S(2)}) collective-permute-start(bf16[82,320]{0,1:T(8,128)(2,1)S(1)} %get-tuple-element.14), channel_id=1, source_target_pairs={{0,1},{2,3},{4,5},{6,7},{8,9},{10,11},{12,13},{14,15},{16,17},{18,... | collective-permute-start | bytes 157448 | tf_op jit(solution)/shard_map/ppermute | solution.py:16
  21.1 1.3 collective-permute-start.1
  22.4 4.5 %copy.84 = bf16[10,384,256]{2,0,1:T(8,128)(2,1)} copy(bf16[10,384,256]{2,1,0:T(8,128)(2,1)} %param.6) | data formatting | bytes 3932160 | tf_op args[0]
  26.9 4.7 %all-to-all-start = ((bf16[10,384,256]{2,0,1:T(8,128)(2,1)}), bf16[10,384,256]{2,0,1:T(8,128)(2,1)}, u32[]{:S(2)}, u32[]{:S(2)}) async-start(bf16[10,384,256]{2,0,1:T(8,128)(2,1)} %copy.84), calls=%async_computation | async-start | bytes 6291456 | tf_op jit(solution)/shard_map/all_to_all | solution.py:102
  31.6 0.8 compare_and_fusion
  32.4 0.8 add_multiply_fusion
  33.2 0.0 collective-permute-done
  33.2 0.0 collective-permute-done.1
  33.2 0.1 pad_maximum_fusion
  33.3 18.1 %gather_fusion = bf16[6144,82]{1,0:T(8,128)(2,1)S(1)} fusion(bf16[82,1024]{0,1:T(8,128)(2,1)S(1)} %pad_maximum_fusion, s32[6144]{0:T(1024)S(1)} %broadcast_clamp_fusion), kind=kCustom, calls=%fused_computation | custom fusion | bytes 2039808 | tf_op jit(solution)/shard_map/jit(_take)/gather | solution.py:66
  51.4 0.9 copy.69
  52.4 0.1 select_convert_fusion
  52.5 0.2 slice_reduce_fusion
  52.7 0.1 fusion.69
  52.8 1.8 multiply_reduce_fusion
  54.5 0.2 multiply_reduce_fusion.1
  54.7 0.6 fusion.70
  56.0 56.4 %all-reduce = (f32[]{:T(128)}, f32[]{:T(128)}) all-reduce(f32[]{:T(128)S(6)} %div.56, f32[]{:T(128)} %get-tuple-element.5), channel_id=1, replica_groups=mesh['region'=2,'member'=8,'space'=2] {'member','space'}, use_global_device_ids=true, to_apply=%region_3.4 | all-reduce | flops 2 | bytes 16 | tf_op jit(solution)/shard_map/psum | solution.py:99
  113.7 7.0 %abs_reduce_fusion = (f32[80,48]{0,1:T(8,128)S(1)}, f32[48,80,80]{2,1,0:T(8,128)}) fusion(f32[80,80]{0,1:T(8,128)S(1)} %fusion.65, f32[80,48,128]{2,1,0:T(8,128)} %get-tuple-element.10, f32[80,48,128]{2,1,0:T(8,128)S(1)} %get-tuple-element.11), kind=kOutput, calls=%fused_computation.40 | convolution fusion | flops 472776960 | bytes 5201920 | tf_op jit(solution)/shard_map/ank,bnk->abn/dot_general | solution.py:42
  120.7 0.1 reduce_max.9
  120.8 3.6 %fusion.61 = f32[48,80,80]{2,1,0:T(8,128)S(1)} fusion(f32[80,80]{0,1:T(8,128)S(1)} %fusion.67, f32[48,80,80]{2,1,0:T(8,128)} %get-tuple-element.17, f32[48]{0:T(128)S(1)} %reduce_max.9, f32[80,80]{0,1:T(8,128)S(1)} %fusion.65), kind=kOutput, calls=%fused_computation.71 | convolution fusion | flops 295526400 | bytes 2508992 | tf_op jit(solution)/shard_map/abn,bcn->acn/dot_general | solution.py:49
  124.4 0.0 copy-start.2
  124.4 1.8 fusion.34
  126.2 0.0 copy-done.2
  126.2 2.4 %fusion.33 = f32[48,80,80]{2,1,0:T(8,128)S(1)} fusion(f32[48,80,80]{2,1,0:T(8,128)S(1)} %fusion.61, f32[80,80]{0,1:T(8,128)S(1)} %fusion.66, f32[48,80,80]{2,1,0:T(8,128)S(1)} %copy-done.2, f32[48]{0:T(128)S(1)} %reduce_max.9, f32[80,80]{0,1:T(8,128)S(1)} %fusion.65), kind=kOutput, calls=%fused_computation.45 | convolution fusion | flops 296140800 | bytes 3737792 | tf_op jit(solution)/shard_map/abn,bcn->acn/dot_general | solution.py:52
  128.6 0.0 copy-start.1
  128.6 2.4 %fusion.19 = f32[48,80,80]{2,1,0:T(8,128)S(1)} fusion(f32[48,80,80]{2,1,0:T(8,128)S(1)} %fusion.33, f32[48,80,80]{2,1,0:T(8,128)S(1)} %fusion.34), kind=kOutput, calls=%fused_computation.24 | convolution fusion | flops 294912000 | bytes 3686400 | tf_op jit(solution)/shard_map/abn,bcn->acn/dot_general | solution.py:49
  131.0 0.0 copy-done.1
  131.0 0.0 copy-start
  131.1 2.2 fusion.21
  133.2 0.0 copy-done
  133.3 0.1 copy.103
  133.3 4.3 %fusion.17 = f32[48,80,80]{2,1,0:T(8,128)S(1)} fusion(f32[48,80,80]{2,1,0:T(8,128)} %copy-done.1, f32[48,80,80]{2,1,0:T(8,128)} %copy-done, f32[80,80]{0,1:T(8,128)S(1)} %fusion.66), kind=kOutput, calls=%fused_computation.22 | convolution fusion | flops 295526400 | bytes 3712000 | tf_op jit(solution)/shard_map/abn,bcn->acn/dot_general | solution.py:52
  137.7 2.2 fusion.12
  139.9 2.3 %fusion.14 = f32[48,80,80]{2,1,0:T(8,128)S(1)} fusion(f32[48,80,80]{2,1,0:T(8,128)S(1)} %fusion.21, f32[48,80,80]{2,1,0:T(8,128)S(1)} %fusion.12, f32[80,80]{0,1:T(8,128)S(1)} %fusion.66), kind=kOutput, calls=%fused_computation.18 | convolution fusion | flops 295526400 | bytes 3712000 | tf_op jit(solution)/shard_map/abn,bcn->acn/dot_general | solution.py:53
  142.1 2.5 %fusion.10 = f32[48,80,80]{2,1,0:T(8,128)S(1)} fusion(f32[48,80,80]{2,1,0:T(8,128)S(1)} %fusion.17, f32[48,80,80]{2,1,0:T(8,128)S(1)} %fusion.12, f32[80,80]{0,1:T(8,128)S(1)} %fusion.66), kind=kOutput, calls=%fused_computation.14 | convolution fusion | flops 295526400 | bytes 3712000 | tf_op jit(solution)/shard_map/abn,bcn->acn/dot_general | solution.py:52
  144.7 2.2 fusion.6
  146.9 3.5 %fusion.36 = f32[48,80,80]{1,2,0:T(8,128)S(1)} fusion(f32[48,80,80]{2,1,0:T(8,128)S(1)} %fusion.6, f32[48,80,80]{2,1,0:T(8,128)S(1)} %fusion.14, f32[48]{0:T(128)S(1)} %sqrt.7, f32[80,80]{0,1:T(8,128)S(1)} %fusion.66), kind=kOutput, calls=%fused_computation.48 | convolution fusion | flops 295833600 | bytes 3712192 | tf_op jit(solution)/shard_map/abn,bcn->acn/dot_general | solution.py:53
  150.4 3.2 %fusion.39 = f32[80,48,1]{0,2,1:T(1,128)S(1)} fusion(f32[80,48,1]{0,2,1:T(1,128)S(1)} %copy.103, f32[48,80,80]{1,2,0:T(8,128)S(1)} %fusion.36), kind=kOutput, calls=%fused_computation.49 | convolution fusion | flops 3686400 | bytes 1259520 | tf_op jit(solution)/shard_map/abn,bn->an/dot_general | solution.py:56
  153.5 3.2 %fusion = f32[48,1,80]{2,1,0:T(1,128)S(1)} fusion(f32[80,48,1]{0,2,1:T(1,128)S(1)} %fusion.39, f32[48,80,80]{1,2,0:T(8,128)S(1)} %fusion.36), kind=kOutput, calls=%fused_computation.1 | convolution fusion | flops 3686400 | bytes 1259520 | tf_op jit(solution)/shard_map/abn,bn->an/dot_general | solution.py:57
  156.7 0.6 fusion.35
  157.3 0.0 all-to-all-done
  157.3 2.6 %copy.86 = bf16[8,10,48,256]{3,2,1,0:T(8,128)(2,1)S(1)} copy(bf16[8,10,48,256]{3,1,2,0:T(8,128)(2,1)} %bitcast.32) | data formatting | bytes 3932160 | tf_op jit(solution)/shard_map/all_to_all | solution.py:102
  160.0 2.3 %convert_bitcast_fusion = bf16[80,48,256]{2,0,1:T(8,128)(2,1)S(1)} fusion(bf16[80,48,256]{2,1,0:T(8,128)(2,1)S(1)} %bitcast.116, f32[48,80,80]{1,2,0:T(8,128)S(1)} %fusion.36, f32[80,48]{0,1:T(8,128)S(1)} %broadcast_multiply_fusion.1, f32[80,48]{0,1:T(8,128)S(1)} %bitcast.120), kind=kOutput, calls=%fused_computation.36 | convolution fusion | flops 159805440 | bytes 5191680 | tf_op jit(solution)/shard_map/inc,ijn->jnc/dot_general | solution.py:105
  162.3 0.7 copy.89
  162.9 58.4 %all_to_all.36 = bf16[80,48,256]{2,1,0:T(8,128)(2,1)S(1)} all-to-all(bf16[80,48,256]{2,1,0:T(8,128)(2,1)S(1)} %copy.89), channel_id=1, replica_groups=mesh['region'=2,'member'=8,'space'=2] {'member'}, dimensions={0} | all-to-all | bytes 3932160 | tf_op jit(solution)/shard_map/all_to_all | solution.py:108
  221.3 1.5 copy.90
  (11 shorter events, 0.1 us)
Async XLA Ops:
  17.7 15.5 %collective-permute-start = (bf16[82,320]{0,1:T(8,128)(2,1)S(1)}, bf16[82,320]{0,1:T(8,128)(2,1)S(1)}, u32[]{:S(2)}, u32[]{:S(2)}) collective-permute-start(bf16[82,320]{0,1:T(8,128)(2,1)S(1)} %get-tuple-element.14), channel_id=1, source_target_pairs={{0,1},{2,3},{4,5},{6,7},{8,9},{10,11},{12,13},{14,15},{16,17},{18,... | collective-permute-start | bytes 157448 | tf_op jit(solution)/shard_map/ppermute | solution.py:16
  21.1 12.1 %collective-permute-start.1 = (bf16[82,320]{0,1:T(8,128)(2,1)S(1)}, bf16[82,320]{0,1:T(8,128)(2,1)S(1)}, u32[]{:S(2)}, u32[]{:S(2)}) collective-permute-start(bf16[82,320]{0,1:T(8,128)(2,1)S(1)} %get-tuple-element.15), channel_id=1, source_target_pairs={{1,0},{3,2},{5,4},{7,6},{9,8},{11,10},{13,12},{15,14},{17,16},{19,... | collective-permute-start | bytes 157448 | tf_op jit(solution)/shard_map/ppermute | solution.py:17
  26.9 130.4 %all-to-all-start = ((bf16[10,384,256]{2,0,1:T(8,128)(2,1)}), bf16[10,384,256]{2,0,1:T(8,128)(2,1)}, u32[]{:S(2)}, u32[]{:S(2)}) async-start(bf16[10,384,256]{2,0,1:T(8,128)(2,1)} %copy.84), calls=%async_computation | async-start | bytes 6291456 | tf_op jit(solution)/shard_map/all_to_all | solution.py:102
  124.4 1.8 copy-start.2
  128.6 2.4 %copy-start.1 = (f32[48,80,80]{2,1,0:T(8,128)}, f32[48,80,80]{2,1,0:T(8,128)S(1)}, u32[]{:S(2)}) copy-start(f32[48,80,80]{2,1,0:T(8,128)S(1)} %fusion.33) | copy-start | bytes 3686404
  131.0 2.2 copy-start
where the time goes:
time: 227 us; the launch traced here: 223 us
  blocking collectives  131 us (58%)
  matrix products  45 us (20%)
  local copies, waits for them, and re-layouts  30.1 us (13%)
  starting transfers between devices  9.35 us (4%)
  other arithmetic  5.51 us (2%)
  between operations  2.5 us (1%)
    all_to_all x1, blocking collectives, per_device(): lax.all_to_all(updated, 'member', split_axis=0, concat_axis=1, tiled=True)  58.4 us
    psum x1, blocking collectives, per_device(): fit_sum, spread = lax.psum((fit_sum, spread), ('member', 'space'))  56.4 us
    gather x2, local copies, waits for them, and re-layouts, select_domains(): jnp.take(window, obs_lists.reshape(-1), axis=1)  19 us
    all_gather x1, blocking collectives, per_device(): gathered = lax.all_gather(prior_at_sensors, 'member', axis=0, tiled=True)  15.8 us
    dot_general x4, matrix products, transform(): jnp.einsum('abn,bcn->acn', inverse, root_iter, precision=exact)  10.4 us
    dot_general x4, matrix products, transform(): inverse = jnp.einsum('abn,bcn->acn', factor, inverse, precision=exact)  9.78 us
    dot_general x3, matrix products, transform(): root_iter = jnp.einsum('abn,bcn->acn', root_iter, factor, precision=exact)  9.26 us
    dot_general x1, matrix products, transform(): gram = jnp.einsum('ank,bnk->abn', weighted, anomaly, precision=exact)  7.01 us
  transfers between devices with their start and end apart: 3, of which 0 were waited for; matrix products, arithmetic and copies ran while one was open for 32% of the time, Pallas kernels for 0%

commit v1 on v0

v1 whole, which is shorter than its diff:
```python
import functools

import jax
import jax.numpy as jnp
from jax import lax
from jax.experimental import pallas as pl
from jax.experimental.pallas import tpu as pltpu
from jax.sharding import PartitionSpec as P

NS_STEPS = 4
LANES = 128
GROUP = 4
MESH = pl.DeviceIdType.MESH
F32 = jnp.float32
BF16 = jnp.bfloat16


def partner(me, k, n):
    if n & (n - 1):
        return lax.rem(me + k, n)
    other, bit = me, 1
    while bit < n:
        if k & bit:
            other = other + bit * (1 - 2 * lax.rem(me // bit, 2))
        bit *= 2
    return other


def split(value):
    high = value.astype(BF16)
    return high, (value - high.astype(F32)).astype(BF16)


def times(left, right):
    lh, ll = split(left)
    rh, rl = split(right)
    rows, k = left.shape[0], right.shape[0]
    lhs = jnp.concatenate([lh, ll], axis=0)[:, :k]
    rhs = jnp.concatenate([rh, rl], axis=1)
    out = jnp.dot(lhs, rhs, preferred_element_type=F32)
    width = right.shape[1]
    return out[:rows, :width] + out[:rows, width:] + out[rows:, :width]


def analyse_kernel(
    n, spaces, halo, obs_count, x, pack, lists, radius,
    incoming, trans_out,
    gathered, full, anoms, anoms_t, marks, weights, gram, target, moved, sums, sums2,
    bulk_send, bulk_recv, local_sem, side_send, side_recv, sum_send, sum_recv, sum2_send, sum2_recv,
):
    me = lax.axis_index("member")
    space = lax.axis_index("space")
    members, patch, _ = x.shape
    domains = patch // n
    lines = members * n
    width = anoms.shape[1]

    barrier = pltpu.get_barrier_semaphore()

    def greet(k, carry):
        other = lax.rem(me + space * n + k, n * spaces)
        pl.semaphore_signal(
            barrier, inc=1,
            device_id={"member": lax.rem(other, n), "space": other // n},
            device_id_type=MESH,
        )
        return carry

    lax.fori_loop(1, n * spaces, greet, 0)
    pl.semaphore_wait(barrier, n * spaces - 1)

    def side_copy(side, k):
        to_space = lax.rem(space + 1 - side + spaces, spaces)
        to = partner(me, k, n)
        return pltpu.make_async_remote_copy(
            pack, gathered.at[side, me], side_send.at[side, k], side_recv.at[side, k],
            device_id={"member": to, "space": to_space}, device_id_type=MESH,
        )

    has_left, has_right = space > 0, space < spaces - 1
    for k in range(1, n):
        side_copy(1, k).start()

    @pl.when(has_right)
    def _():
        for k in range(n):
            side_copy(0, k).start()

    @pl.when(has_left)
    def _():
        for k in range(n):
            side_copy(2, k).start()

    bulk = []
    for k in range(1, n):
        to = partner(me, k, n)
        copy = pltpu.make_async_remote_copy(
            x.at[:, pl.ds(pl.multiple_of(to * domains, 16), domains), :],
            incoming.at[pl.ds(me * members, members)],
            bulk_send.at[k], bulk_recv.at[k],
            device_id={"member": to}, device_id_type=MESH,
        )
        copy.start()
        bulk.append(copy)
    own = pltpu.make_async_copy(
        x.at[:, pl.ds(pl.multiple_of(me * domains, 16), domains), :],
        incoming.at[pl.ds(me * members, members)], local_sem,
    )
    own.start()

    gathered[1, me] = pack[...]

    @pl.when(space == 0)
    def _():
        gathered[0] = jnp.ones(gathered.shape[1:], BF16)

    @pl.when(space == spaces - 1)
    def _():
        gathered[2] = jnp.ones(gathered.shape[1:], BF16)

    lane = lax.broadcasted_iota(jnp.int32, (obs_count, width), 1)

    def mark(group, carry):
        start = pl.multiple_of(group * 8, 8)
        columns = jnp.transpose(lists[pl.ds(start, 8), :] - me * domains)
        rows = []
        for d in range(8):
            hit = columns[:, d : d + 1] == lane
            rows.append(jnp.sum(jnp.where(hit, 1.0, 0.0), axis=0, keepdims=True))
        marks[pl.ds(start, 8), :] = jnp.concatenate(rows, axis=0)
        return carry

    lax.fori_loop(0, domains // 8, mark, 0)

    for k in range(1, n):
        side_copy(1, k).wait()

    @pl.when(has_right)
    def _():
        for k in range(n):
            side_copy(0, k).wait_send()
            side_copy(2, k).wait_recv()

    @pl.when(has_left)
    def _():
        for k in range(n):
            side_copy(2, k).wait_send()
            side_copy(0, k).wait_recv()

    for side in range(3):
        for s in range(n):
            full[members * s : members * (s + 1), patch * side : patch * (side + 1)] = (
                gathered[side, s, :members, :].astype(F32)
            )
        full[lines : lines + 2, patch * side : patch * (side + 1)] = (
            gathered[side, 0, members : members + 2, :].astype(F32)
        )
    total = 3 * patch
    shift = lax.rem(2 * total - (patch - halo) - me * domains, total)
    turned = pltpu.roll(full[...], shift, 1)[:, :width]
    values = turned[:lines]
    mean = jnp.sum(values, axis=0, keepdims=True) * (1.0 / lines)
    anomaly = values - mean
    anoms[...] = anomaly
    innov = turned[lines : lines + 1] - mean
    noise = turned[lines + 1 : lines + 2]
    squares = jnp.sum(anomaly * anomaly, axis=0, keepdims=True)

    place = lax.broadcasted_iota(jnp.int32, (domains, width), 1)
    row = lax.broadcasted_iota(jnp.int32, (domains, width), 0)
    distance = jnp.abs(place - halo - row).astype(F32) / radius[...]
    weight = marks[...] * jnp.exp(-2.0 * distance * distance) / noise
    weights[...] = weight
    fit = jnp.sum(weight * (innov * innov))
    spread = jnp.sum(weight * squares)
    first = lax.broadcasted_iota(jnp.int32, (8, LANES), 0) == 0
    moved[0] = jnp.where(first, fit, spread)

    high, low = split(anomaly)
    pad = jnp.zeros((LANES - lines, width), F32)
    anoms_t[...] = jnp.concatenate(
        [
            jnp.transpose(jnp.concatenate([high.astype(F32), pad], axis=0)),
            jnp.transpose(jnp.concatenate([low.astype(F32), pad], axis=0)),
        ],
        axis=1,
    ).astype(BF16)

    sum_copies = []
    for k in range(1, n):
        copy = pltpu.make_async_remote_copy(
            moved.at[0], sums.at[k], sum_send.at[k], sum_recv.at[k],
            device_id={"member": partner(me, k, n) if not n & (n - 1) else lax.rem(me + n - k, n)},
            device_id_type=MESH,
        )
        copy.start()
        sum_copies.append(copy)

    def one_gram(c):
        weighted = anoms[...] * weights[pl.ds(c, 1), :]
        hi, lo = split(weighted)
        out = jnp.dot(
            jnp.concatenate([hi, lo], axis=0), anoms_t[...], preferred_element_type=F32
        )
        gram[c] = out[:lines, :LANES] + out[:lines, LANES:] + out[lines:, :LANES]
        aim = jnp.sum(weighted * innov, axis=1, keepdims=True)
        target[c] = jnp.broadcast_to(aim, (lines, LANES))

    def gram_group(g, carry):
        for d in range(2):
            one_gram(g * 2 + d)
        return carry

    half = domains // 4
    lax.fori_loop(0, half, gram_group, 0)

    for copy in sum_copies:
        copy.wait()
    partial = moved[0]
    for k in range(1, n):
        partial = partial + sums[k]
    moved[1] = partial
    sum2_copies = []
    for k in range(1, spaces):
        copy = pltpu.make_async_remote_copy(
            moved.at[1], sums2.at[k], sum2_send.at[k], sum2_recv.at[k],
            device_id={"space": lax.rem(space + k, spaces)}, device_id_type=MESH,
        )
        sum2_copies.append(copy)
    gram_group(half, 0)
    for copy in sum2_copies:
        copy.start()
    lax.fori_loop(half + 1, domains // 2, gram_group, 0)
    for copy in sum2_copies:
        copy.wait()
    for k in range(1, spaces):
        partial = partial + sums2[k]
    scale = (lines - 1.0) * (partial[1:2, :] / (lines - 1.0)) / partial[0:1, :]

    eye = jnp.where(
        lax.broadcasted_iota(jnp.int32, (lines, LANES), 0)
        == lax.broadcasted_iota(jnp.int32, (lines, LANES), 1),
        1.0, 0.0,
    )
    diagonal = eye * scale

    def solve_group(g, carry):
        ids = [g * GROUP + d for d in range(GROUP)]
        mats = [gram[c] + diagonal for c in ids]
        bounds = [
            jnp.max(jnp.sum(jnp.abs(m), axis=0, keepdims=True), axis=1, keepdims=True)
            for m in mats
        ]
        ys = [m / b for m, b in zip(mats, bounds)]
        zs = [1.5 * eye - 0.5 * y for y in ys]
        ys = [times(y, z) for y, z in zip(ys, zs)]
        for step in range(1, NS_STEPS):
            ps = [1.5 * eye - 0.5 * times(z, y) for z, y in zip(zs, ys)]
            if step < NS_STEPS - 1:
                both = [
                    times(jnp.concatenate([y, z], axis=0), p) for y, z, p in zip(ys, zs, ps)
                ]
                ys = [b[:lines] for b in both]
                zs = [b[lines:] for b in both]
            else:
                zs = [times(z, p) for z, p in zip(zs, ps)]
        roots = [z * lax.rsqrt(b) for z, b in zip(zs, bounds)]
        for c, root in zip(ids, roots):
            half_gain = jnp.sum(root * target[c], axis=0, keepdims=True)
            gain = jnp.sum(root * half_gain, axis=1, keepdims=True)
            w = (lines - 1.0) ** 0.5 * root + gain
            w = w - jnp.sum(w, axis=0, keepdims=True) * (1.0 / lines) + 1.0 / lines
            trans_out[c] = w.astype(BF16)
        return carry

    lax.fori_loop(0, domains // GROUP, solve_group, 0)

    own.wait()
    for copy in bulk:
        copy.wait()


def spread_kernel(n, x, out, send, recv, local_sem):
    me = lax.axis_index("member")
    members, domains = x.shape[0] // n, x.shape[1]
    barrier = pltpu.get_barrier_semaphore()
    for k in range(1, n):
        pl.semaphore_signal(
            barrier, inc=1, device_id={"member": lax.rem(me + k, n)}, device_id_type=MESH
        )
    pl.semaphore_wait(barrier, n - 1)
    place = out.at[:, pl.ds(pl.multiple_of(me * domains, 16), domains), :]
    copies = []
    for k in range(1, n):
        to = partner(me, k, n)
        copy = pltpu.make_async_remote_copy(
            x.at[pl.ds(to * members, members)], place, send.at[k], recv.at[k],
            device_id={"member": to}, device_id_type=MESH,
        )
        copy.start()
        copies.append(copy)
    own = pltpu.make_async_copy(x.at[pl.ds(me * members, members)], place, local_sem)
    own.start()
    own.wait()
    for copy in copies:
        copy.wait()


def per_device(trials, sensors, readings, noise, lists, tiers):
    n, spaces = lax.axis_size("member"), lax.axis_size("space")
    members, patch, quantities = trials.shape
    obs_count = lists.shape[1]
    halo = 5 * obs_count // 2
    domains = patch // n
    lines = members * n
    width = -(-(domains + 2 * halo) // 256) * 256
    rows = -(-(members + 2) // 16) * 16
    first_col = lax.axis_index("member") * domains
    own_lists = lax.dynamic_slice_in_dim(lists, first_col, domains, 0)
    own_tiers = lax.dynamic_slice_in_dim(tiers, first_col, domains, 0)
    radius = ((own_tiers.astype(F32) + 2.0) * (0.5 * obs_count))[:, None]
    pack = jnp.concatenate(
        [sensors, readings[None], noise[None], jnp.ones((rows - members - 2, patch), BF16)], axis=0
    )
    vmem = pl.BlockSpec(memory_space=pltpu.VMEM)
    anywhere = pl.BlockSpec(memory_space=pl.ANY)
    full_rows = -(-(lines + 2) // 8) * 8
    dma = pltpu.SemaphoreType.DMA
    incoming, trans = pl.pallas_call(
        functools.partial(analyse_kernel, n, spaces, halo, obs_count),
        out_shape=(
            jax.ShapeDtypeStruct((lines, domains, quantities), BF16),
            jax.ShapeDtypeStruct((domains, lines, LANES), BF16),
        ),
        in_specs=[anywhere, vmem, vmem, vmem],
        out_specs=(anywhere, vmem),
        scratch_shapes=[
            pltpu.VMEM((3, n, rows, patch), BF16),
            pltpu.VMEM((full_rows, 3 * patch), F32),
            pltpu.VMEM((lines, width), F32),
            pltpu.VMEM((width, 2 * LANES), BF16),
            pltpu.VMEM((domains, width), F32),
            pltpu.VMEM((domains, width), F32),
            pltpu.VMEM((domains, lines, LANES), F32),
            pltpu.VMEM((domains, lines, LANES), F32),
            pltpu.VMEM((2, 8, LANES), F32),
            pltpu.VMEM((n, 8, LANES), F32),
            pltpu.VMEM((spaces, 8, LANES), F32),
            dma((n,)), dma((n,)), dma, dma((3, n)), dma((3, n)),
            dma((n,)), dma((n,)), dma((spaces,)), dma((spaces,)),
        ],
        compiler_params=pltpu.CompilerParams(
            collective_id=0, has_side_effects=True, vmem_limit_bytes=40 << 20
        ),
        name="analyse",
    )(trials, pack, own_lists, radius)
    updated = jnp.einsum(
        "inc,nij->jnc", incoming, trans[:, :, :lines], preferred_element_type=F32
    ).astype(BF16)
    return pl.pallas_call(
        functools.partial(spread_kernel, n),
        out_shape=jax.ShapeDtypeStruct((members, patch, quantities), BF16),
        in_specs=[vmem],
        out_specs=anywhere,
        scratch_shapes=[dma((n,)), dma((n,)), dma],
        compiler_params=pltpu.CompilerParams(collective_id=1, has_side_effects=True),
        name="spread",
    )(updated)


def solution(mesh):
    return jax.shard_map(
        per_device,
        mesh=mesh,
        in_specs=(
            P("member", ("region", "space"), None),
            P("member", ("region", "space")),
            P(("region", "space")),
            P(("region", "space")),
            P(("region", "space"), None),
            P(("region", "space")),
        ),
        out_specs=P("member", ("region", "space"), None),
        check_vma=False,
    )
```

time: 227 us -> 135 us (0.59)
  the two profiles are of different devices: /device:TPU:0 before, /device:TPU:13 now
where the time goes in v1:
time: 135 us
  Pallas kernels  124 us (92%)
  local copies, waits for them, and re-layouts  8.02 us (6%)
  other arithmetic  1.58 us (1%)
    pallas_call x1, Pallas kernels, per_device(): pl.pallas_call(functools.partial(analyse_kernel, n, spaces, halo, obs_cou...  76.6 us
    pallas_call x1, Pallas kernels, per_device(): pl.pallas_call(functools.partial(spread_kernel, n), out_shape=jax.ShapeDt...  47.5 us
    unnamed x5, local copies, waits for them, and re-layouts  4.49 us

profile of v1, /device:TPU:13, one launch (start us, length us, event | category | flops | bytes accessed | tf_op | source)
XLA Modules:
  0.0 134.6 jit_solution(14607231208699836991)
XLA Ops:
  0.0 0.0 copy-start
  0.0 0.8 multiply_bitcast_fusion
  0.8 0.1 pad.3.clone
  0.9 0.7 broadcast_in_dim.12
  1.6 0.7 broadcast_in_dim.13
  2.2 0.8 maximum_maximum_fusion.pack
  3.0 0.0 copy-done
  3.0 0.1 copy.7.radius
  3.1 0.0 copy-start.1
  3.1 1.5 %copy-done.1 = bf16[10,384,256]{2,1,0:T(8,128)(2,1)S(1)} copy-done((bf16[10,384,256]{2,1,0:T(8,128)(2,1)S(1)}, bf16[10,384,256]{2,1,0:T(8,128)(2,1)}, u32[]{:S(2)}) %copy-start.1) | copy-done | bytes 1966104
  4.7 76.6 %analyse.1 = (bf16[80,48,256]{2,1,0:T(8,128)(2,1)S(1)}, bf16[48,80,128]{2,1,0:T(8,128)(2,1)S(1)}) custom-call(bf16[10,384,256]{2,1,0:T(8,128)(2,1)S(1)} %copy-done.1, bf16[16,384]{1,0:T(8,128)(2,1)S(1)} %maximum_maximum_fusion.pack, s32[48,128]{1,0:T(8,128)S(1)} %constant_dynamic-slice_fusion.lists, f32[48,1]{1,0:T(8,128)S(1)} %copy.7.radius), custom_call_target="tpu_custom_call" | custom-call | tf_op jit(solution)/shard_map/analyse/pallas_call | solution.py:329
  81.3 0.8 fusion.1
  82.1 2.0 %copy.17 = bf16[48,80,256]{2,0,1:T(8,128)(2,1)} copy(bf16[48,80,256]{2,1,0:T(8,128)(2,1)S(1)} %fusion.1) | data formatting | bytes 3932160 | tf_op jit(solution)/shard_map/inc,nij->jnc/dot_general | solution.py:357
  84.1 47.5 %spread.1 = bf16[10,384,256]{2,1,0:T(8,128)(2,1)} custom-call(bf16[80,48,256]{2,1,0:T(8,128)(2,1)} %bitcast.5), custom_call_target="tpu_custom_call" | custom-call | tf_op jit(solution)/shard_map/spread/pallas_call | solution.py:360
  131.6 2.9 %copy.19 = bf16[10,384,256]{2,1,0:T(8,128)(2,1)} copy(bf16[10,384,256]{2,1,0:T(8,128)(2,1)} %spread.1) | data formatting | bytes 3932160
  (2 shorter events, 0.0 us)
Async XLA Ops:
  0.0 3.0 %copy-start = (s32[384,128]{1,0:T(8,128)S(1)}, s32[384,128]{1,0:T(8,128)}, u32[]{:S(2)}) copy-start(s32[384,128]{1,0:T(8,128)} %param.10) | copy-start | bytes 589828
  3.1 1.5 %copy-start.1 = (bf16[10,384,256]{2,1,0:T(8,128)(2,1)S(1)}, bf16[10,384,256]{2,1,0:T(8,128)(2,1)}, u32[]{:S(2)}) copy-start(bf16[10,384,256]{2,1,0:T(8,128)(2,1)} %x.1) | copy-start | bytes 5898244

commit v2 on v1

v2 whole, which is shorter than its diff:
```python
import functools

import jax
import jax.numpy as jnp
from jax import lax
from jax.experimental import pallas as pl
from jax.experimental.pallas import tpu as pltpu
from jax.sharding import PartitionSpec as P

NS_STEPS = 4
LANES = 128
GROUP = 4
CHUNK = 16
MESH = pl.DeviceIdType.MESH
F32 = jnp.float32
BF16 = jnp.bfloat16


def partner(me, k, n):
    if n & (n - 1):
        return lax.rem(me + k, n)
    other, bit = me, 1
    while bit < n:
        if k & bit:
            other = other + bit * (1 - 2 * lax.rem(me // bit, 2))
        bit *= 2
    return other


def split(value):
    high = value.astype(BF16)
    return high, (value - high.astype(F32)).astype(BF16)


def times(left, right):
    lh, ll = split(left)
    rh, rl = split(right)
    rows, k = left.shape[0], right.shape[0]
    lhs = jnp.concatenate([lh, ll], axis=0)[:, :k]
    rhs = jnp.concatenate([rh, rl], axis=1)
    out = jnp.dot(lhs, rhs, preferred_element_type=F32)
    width = right.shape[1]
    return out[:rows, :width] + out[:rows, width:] + out[rows:, :width]


def analyse_kernel(
    n, spaces, halo, obs_count, x, sensors, readings, noises, lists, tiers,
    out,
    pack, incoming, updated, gathered, full, anoms, anoms_t, marks, weights, gram, target, trans,
    moved, sums,
    in_send, in_recv, out_send, out_recv, local_sem, side_send, side_recv, sum_send, sum_recv,
):
    me = lax.axis_index("member")
    space = lax.axis_index("space")
    members, patch, _ = x.shape
    domains = patch // n
    lines = members * n
    width = anoms.shape[1]
    chunks = domains // CHUNK
    peers = n * spaces

    rows = pack.shape[0]
    pack[...] = jnp.concatenate(
        [
            sensors[...].astype(F32), readings[...].astype(F32), noises[...].astype(F32),
            jnp.ones((rows - members - 2, patch), F32),
        ],
        axis=0,
    ).astype(BF16)

    def peer(k):
        other = lax.rem(me + space * n + k, peers)
        return {"member": lax.rem(other, n), "space": other // n}

    barrier = pltpu.get_barrier_semaphore()

    def greet(k, carry):
        pl.semaphore_signal(barrier, inc=1, device_id=peer(k), device_id_type=MESH)
        return carry

    lax.fori_loop(1, peers, greet, 0)

    lane = lax.broadcasted_iota(jnp.int32, (obs_count, width), 1)

    def mark(group, carry):
        start = pl.multiple_of(group * 8, 8)
        source = pl.multiple_of(me * domains + group * 8, 8)
        columns = jnp.transpose(lists[pl.ds(source, 8), :] - me * domains)
        found = []
        for d in range(8):
            hit = columns[:, d : d + 1] == lane
            found.append(jnp.sum(jnp.where(hit, 1.0, 0.0), axis=0, keepdims=True))
        marks[pl.ds(start, 8), :] = jnp.concatenate(found, axis=0)
        return carry

    pl.semaphore_wait(barrier, peers - 1)

    def side_copy(side, k):
        to_space = lax.rem(space + 1 - side + spaces, spaces)
        return pltpu.make_async_remote_copy(
            pack, gathered.at[side, me], side_send.at[side, k], side_recv.at[side, k],
            device_id={"member": partner(me, k, n), "space": to_space}, device_id_type=MESH,
        )

    has_left, has_right = space > 0, space < spaces - 1
    for k in range(1, n):
        side_copy(1, k).start()

    @pl.when(has_right)
    def _():
        for k in range(n):
            side_copy(0, k).start()

    @pl.when(has_left)
    def _():
        for k in range(n):
            side_copy(2, k).start()

    def in_views(to, g):
        return (
            x.at[:, pl.ds(pl.multiple_of(to * domains + g * CHUNK, 16), CHUNK), :],
            incoming.at[pl.ds(me * members, members), pl.ds(g * CHUNK, CHUNK), :],
        )

    def in_copy(g, k):
        to = partner(me, k, n)
        source, place = in_views(to, g)
        return pltpu.make_async_remote_copy(
            source, place, in_send.at[g, k], in_recv.at[g, k],
            device_id={"member": to}, device_id_type=MESH,
        )

    far_first = list(range(n // 2, n)) + list(range(1, n // 2))
    pairs = [(g, k) for g in range(chunks) for k in far_first]
    early = n // 2 - 1
    for g, k in pairs[:early]:
        in_copy(g, k).start()
    own = []
    for g in range(chunks):
        source, place = in_views(me, g)
        copy = pltpu.make_async_copy(source, place, local_sem.at[0, g])
        copy.start()
        own.append(copy)

    gathered[1, me] = pack[...]

    @pl.when(space == 0)
    def _():
        gathered[0] = jnp.ones(gathered.shape[1:], BF16)

    @pl.when(space == spaces - 1)
    def _():
        gathered[2] = jnp.ones(gathered.shape[1:], BF16)

    lax.fori_loop(0, domains // 8, mark, 0)

    for k in range(1, n):
        side_copy(1, k).wait()

    @pl.when(has_right)
    def _():
        for k in range(n):
            side_copy(0, k).wait_send()
            side_copy(2, k).wait_recv()

    @pl.when(has_left)
    def _():
        for k in range(n):
            side_copy(2, k).wait_send()
            side_copy(0, k).wait_recv()

    for side in range(3):
        for s in range(n):
            full[members * s : members * (s + 1), patch * side : patch * (side + 1)] = (
                gathered[side, s, :members, :].astype(F32)
            )
        full[lines : lines + 2, patch * side : patch * (side + 1)] = (
            gathered[side, 0, members : members + 2, :].astype(F32)
        )
    total = 3 * patch
    shift = lax.rem(2 * total - (patch - halo) - me * domains, total)
    turned = pltpu.roll(full[...], shift, 1)[:, :width]
    values = turned[:lines]
    mean = jnp.sum(values, axis=0, keepdims=True) * (1.0 / lines)
    anomaly = values - mean
    anoms[...] = anomaly
    innov = turned[lines : lines + 1] - mean
    noise = turned[lines + 1 : lines + 2]
    squares = jnp.sum(anomaly * anomaly, axis=0, keepdims=True)

    own_tier = lax.broadcasted_iota(jnp.int32, (domains, patch), 1) == (
        lax.broadcasted_iota(jnp.int32, (domains, patch), 0) + me * domains
    )
    tier = jnp.sum(jnp.where(own_tier, tiers[...].astype(F32), 0.0), axis=1, keepdims=True)
    radius = (tier + 2.0) * (0.5 * obs_count)
    place = lax.broadcasted_iota(jnp.int32, (domains, width), 1)
    row = lax.broadcasted_iota(jnp.int32, (domains, width), 0)
    distance = jnp.abs(place - halo - row).astype(F32) / radius
    weight = marks[...] * jnp.exp(-2.0 * distance * distance) / noise
    weights[...] = weight
    fit = jnp.sum(weight * (innov * innov))
    spread = jnp.sum(weight * squares)
    first = lax.broadcasted_iota(jnp.int32, (8, LANES), 0) == 0
    moved[...] = jnp.where(first, fit, spread)

    high, low = split(anomaly)
    pad = jnp.zeros((LANES - lines, width), F32)
    anoms_t[...] = jnp.concatenate(
        [
            jnp.transpose(jnp.concatenate([high.astype(F32), pad], axis=0)),
            jnp.transpose(jnp.concatenate([low.astype(F32), pad], axis=0)),
        ],
        axis=1,
    ).astype(BF16)

    def sum_copy(k):
        return pltpu.make_async_remote_copy(
            moved, sums.at[k], sum_send.at[k], sum_recv.at[k],
            device_id=peer(k), device_id_type=MESH,
        )

    def start_sum(k, carry):
        sum_copy(k).start()
        return carry

    def end_sum(k, carry):
        sum_copy(k).wait()
        return carry + sums[k]

    lax.fori_loop(1, peers, start_sum, 0)
    for g, k in pairs[early:]:
        in_copy(g, k).start()

    hi, lo = split(weight * innov)
    aims = jnp.dot(jnp.concatenate([hi, lo], axis=0), anoms_t[...], preferred_element_type=F32)
    target[...] = aims[:domains, :LANES] + aims[:domains, LANES:] + aims[domains:, :LANES]

    def gram_group(g, carry):
        for d in range(2):
            c = g * 2 + d
            hi, lo = split(anoms[...] * weights[pl.ds(c, 1), :])
            prod = jnp.dot(
                jnp.concatenate([hi, lo], axis=0), anoms_t[...], preferred_element_type=F32
            )
            gram[c] = prod[:lines, :LANES] + prod[:lines, LANES:] + prod[lines:, :LANES]
        return carry

    lax.fori_loop(0, domains // 2, gram_group, 0)

    sums_all = lax.fori_loop(1, peers, end_sum, moved[...])
    scale = sums_all[1:2, :] / sums_all[0:1, :]
    eye = jnp.where(
        lax.broadcasted_iota(jnp.int32, (lines, LANES), 0)
        == lax.broadcasted_iota(jnp.int32, (lines, LANES), 1),
        1.0, 0.0,
    )
    diagonal = eye * scale

    def solve_group(g, carry):
        ids = [g * GROUP + d for d in range(GROUP)]
        mats = [gram[c] + diagonal for c in ids]
        bounds = [
            jnp.max(jnp.sum(jnp.abs(m), axis=0, keepdims=True), axis=1, keepdims=True)
            for m in mats
        ]
        ys = [m / b for m, b in zip(mats, bounds)]
        zs = [1.5 * eye - 0.5 * y for y in ys]
        ys = [times(y, z) for y, z in zip(ys, zs)]
        for step in range(1, NS_STEPS):
            ps = [1.5 * eye - 0.5 * times(z, y) for z, y in zip(zs, ys)]
            if step < NS_STEPS - 1:
                both = [
                    times(jnp.concatenate([y, z], axis=0), p) for y, z, p in zip(ys, zs, ps)
                ]
                ys = [b[:lines] for b in both]
                zs = [b[lines:] for b in both]
            else:
                zs = [times(z, p) for z, p in zip(zs, ps)]
        roots = [z * lax.rsqrt(b) for z, b in zip(zs, bounds)]
        for c, root in zip(ids, roots):
            half_gain = jnp.sum(root * target[pl.ds(c, 1), :], axis=1, keepdims=True)
            gain = jnp.sum(root * half_gain, axis=0, keepdims=True)
            w = (lines - 1.0) ** 0.5 * root + gain
            w = w - jnp.sum(w, axis=1, keepdims=True) * (1.0 / lines) + 1.0 / lines
            trans[c] = w.astype(BF16)
        return carry

    def out_views(to, g):
        return (
            updated.at[pl.ds(to * members, members), pl.ds(g * CHUNK, CHUNK), :],
            out.at[:, pl.ds(pl.multiple_of(me * domains + g * CHUNK, 16), CHUNK), :],
        )

    def out_copy(g, k):
        to = partner(me, k, n)
        source, place = out_views(to, g)
        return pltpu.make_async_remote_copy(
            source, place, out_send.at[g, k], out_recv.at[g, k],
            device_id={"member": to}, device_id_type=MESH,
        )

    for g in range(chunks):
        lax.fori_loop(g * CHUNK // GROUP, (g + 1) * CHUNK // GROUP, solve_group, 0)
        own[g].wait()
        for k in range(1, n):
            in_copy(g, k).wait()
        states = jnp.swapaxes(incoming[:, g * CHUNK : (g + 1) * CHUNK, :].astype(F32), 0, 1)
        states = states.astype(BF16)
        results = [
            jnp.dot(trans[g * CHUNK + c][:, :lines], states[c], preferred_element_type=F32)
            for c in range(CHUNK)
        ]
        results = jnp.stack(results, axis=0)
        updated[:, g * CHUNK : (g + 1) * CHUNK, :] = jnp.swapaxes(results, 0, 1).astype(BF16)
        for k in far_first:
            out_copy(g, k).start()
        source, place = out_views(me, g)
        copy = pltpu.make_async_copy(source, place, local_sem.at[1, g])
        copy.start()
        own.append(copy)

    for g in range(chunks):
        own[chunks + g].wait()
        for k in range(1, n):
            out_copy(g, k).wait()


def per_device(trials, sensors, readings, noises, lists, tiers):
    n, spaces = lax.axis_size("member"), lax.axis_size("space")
    members, patch, quantities = trials.shape
    obs_count = lists.shape[1]
    halo = 5 * obs_count // 2
    domains = patch // n
    chunks = domains // CHUNK
    lines = members * n
    width = -(-(domains + 2 * halo) // 256) * 256
    rows = -(-(members + 2) // 16) * 16
    vmem = pl.BlockSpec(memory_space=pltpu.VMEM)
    anywhere = pl.BlockSpec(memory_space=pl.ANY)
    full_rows = -(-(lines + 2) // 8) * 8
    dma = pltpu.SemaphoreType.DMA
    return pl.pallas_call(
        functools.partial(analyse_kernel, n, spaces, halo, obs_count),
        out_shape=jax.ShapeDtypeStruct((members, patch, quantities), BF16),
        in_specs=[anywhere] + [vmem] * 5,
        out_specs=vmem,
        scratch_shapes=[
            pltpu.VMEM((rows, patch), BF16),
            pltpu.VMEM((lines, domains, quantities), BF16),
            pltpu.VMEM((lines, domains, quantities), BF16),
            pltpu.VMEM((3, n, rows, patch), BF16),
            pltpu.VMEM((full_rows, 3 * patch), F32),
            pltpu.VMEM((lines, width), F32),
            pltpu.VMEM((width, 2 * LANES), BF16),
            pltpu.VMEM((domains, width), F32),
            pltpu.VMEM((domains, width), F32),
            pltpu.VMEM((domains, lines, LANES), F32),
            pltpu.VMEM((domains, LANES), F32),
            pltpu.VMEM((domains, lines, LANES), BF16),
            pltpu.VMEM((8, LANES), F32),
            pltpu.VMEM((n * spaces, 8, LANES), F32),
            dma((chunks, n)), dma((chunks, n)), dma((chunks, n)), dma((chunks, n)),
            dma((2, chunks)), dma((3, n)), dma((3, n)), dma((n * spaces,)), dma((n * spaces,)),
        ],
        compiler_params=pltpu.CompilerParams(
            collective_id=0, has_side_effects=True, vmem_limit_bytes=48 << 20
        ),
        name="analyse",
    )(trials, sensors, readings[None], noises[None], lists, tiers[None])


def solution(mesh):
    return jax.shard_map(
        per_device,
        mesh=mesh,
        in_specs=(
            P("member", ("region", "space"), None),
            P("member", ("region", "space")),
            P(("region", "space")),
            P(("region", "space")),
            P(("region", "space"), None),
            P(("region", "space")),
        ),
        out_specs=P("member", ("region", "space"), None),
        check_vma=False,
    )
```

time: 135 us -> 104 us (0.77)
  Pallas kernels: 124 us -> 96.9 us
  other arithmetic: 1.58 us -> 0 us
  local copies, waits for them, and re-layouts: 8.02 us -> 6.5 us
    pallas_call x1 -> x0, Pallas kernels: 47.5 us -> none  [per_device(): pl.pallas_call(functools.partial(spread_kernel, n), out_shape=jax.ShapeDt...]
    pallas_call x1, Pallas kernels: 76.6 us -> 96.9 us  [per_device(): pl.pallas_call(functools.partial(analyse_kernel, n, spaces, halo, obs_cou...]
    dot_general x1 -> x0, local copies, waits for them, and re-layouts: 1.99 us -> none  [per_device(): jnp.einsum('inc,nij->jnc', incoming, trans[:, :, :lines], preferred_eleme...]
    unnamed x5 -> x7, local copies, waits for them, and re-layouts: 4.49 us -> 4.45 us
where the time goes in v2:
time: 104 us; the launch traced here: 103 us
  Pallas kernels  96.9 us (93%)
  local copies, waits for them, and re-layouts  6.5 us (6%)
    pallas_call x1, Pallas kernels, per_device(): pl.pallas_call(functools.partial(analyse_kernel, n, spaces, halo, obs_cou...  96.9 us
    unnamed x7, local copies, waits for them, and re-layouts  4.45 us

profile of v2, /device:TPU:13, one launch (start us, length us, event | category | flops | bytes accessed | tf_op | source)
XLA Modules:
  0.0 103.4 jit_solution(1199057330675323116)
XLA Ops:
  0.0 0.7 broadcast_in_dim.9.readings
  0.7 0.7 broadcast_in_dim.10.noises
  1.4 0.7 broadcast_in_dim.11.tiers
  2.0 0.0 copy-start
  2.0 1.5 %copy-done = bf16[10,384,256]{2,1,0:T(8,128)(2,1)S(1)} copy-done((bf16[10,384,256]{2,1,0:T(8,128)(2,1)S(1)}, bf16[10,384,256]{2,1,0:T(8,128)(2,1)}, u32[]{:S(2)}) %copy-start) | copy-done | bytes 1966104
  3.6 0.0 copy-start.1
  3.6 0.9 copy-done.1
  4.5 0.0 copy-start.2
  4.5 0.7 copy-done.2
  5.2 96.9 %analyse.1 = bf16[10,384,256]{2,1,0:T(8,128)(2,1)S(1)} custom-call(bf16[10,384,256]{2,1,0:T(8,128)(2,1)S(1)} %copy-done, bf16[10,384]{1,0:T(8,128)(2,1)S(1)} %copy-done.2, bf16[1,384]{1,0:T(2,128)(2,1)S(1)} %broadcast_in_dim.9.readings, bf16[1,384]{1,0:T(2,128)(2,1)S(1)} %broadcast_in_dim.10.noises, s32[384,128]{1,0:T(8,128)S(1)} %copy-done.1, ...), custom_call_target="tpu_custom_call" | custom-call | tf_op jit(solution)/shard_map/analyse/pallas_call | solution.py:342
  102.1 1.3 %copy.8 = bf16[10,384,256]{2,1,0:T(8,128)(2,1)} copy(bf16[10,384,256]{2,1,0:T(8,128)(2,1)S(1)} %analyse.1) | data formatting | bytes 3932160
Async XLA Ops:
  2.0 1.5 %copy-start = (bf16[10,384,256]{2,1,0:T(8,128)(2,1)S(1)}, bf16[10,384,256]{2,1,0:T(8,128)(2,1)}, u32[]{:S(2)}) copy-start(bf16[10,384,256]{2,1,0:T(8,128)(2,1)} %x.1) | copy-start | bytes 5898244
  3.6 0.9 copy-start.1
  4.5 0.7 copy-start.2

commit v3 on v2

--- a/solution.py
+++ b/solution.py
@@ -44,11 +44,11 @@
 
 
 def analyse_kernel(
-    n, spaces, halo, obs_count, x, sensors, readings, noises, lists, tiers,
+    n, spaces, halo, obs_count, x, sensors_in, readings_in, noises_in, lists_in, tiers_in,
     out,
-    pack, incoming, updated, gathered, full, anoms, anoms_t, marks, weights, gram, target, trans,
+    sensors, readings, noises, lists, tiers, small_sem, pack, incoming, updated, gathered, full, anoms, anoms_t, marks, weights, gram, target, trans,
     moved, sums,
-    in_send, in_recv, out_send, out_recv, local_sem, side_send, side_recv, sum_send, sum_recv,
+    in_send, in_recv, out_send, out_recv, local_sem, cross_send, cross_recv, side_send, side_recv, sum_send, sum_recv,
 ):
     me = lax.axis_index("member")
     space = lax.axis_index("space")
@@ -59,33 +59,47 @@
     chunks = domains // CHUNK
     peers = n * spaces
 
+    small = [
+        pltpu.make_async_copy(source, place, small_sem.at[i])
+        for i, (source, place) in enumerate(
+            [
+                (sensors_in, sensors), (readings_in, readings), (noises_in, noises),
+                (lists_in.at[pl.ds(pl.multiple_of(me * domains, 8), domains)], lists),
+                (tiers_in, tiers),
+            ]
+        )
+    ]
+    for copy in small:
+        copy.start()
+
+    def peer(k):
+        other = lax.rem(me + space * n + k, peers)
+        return {"member": lax.rem(other, n), "space": other // n}
+
+    barrier = pltpu.get_barrier_semaphore()
+
+    def greet(k, carry):
+        pl.semaphore_signal(barrier, inc=1, device_id=peer(k), device_id_type=MESH)
+        return carry
+
+    lax.fori_loop(1, peers, greet, 0)
+    for copy in small:
+        copy.wait()
     rows = pack.shape[0]
     pack[...] = jnp.concatenate(
         [
-            sensors[...].astype(F32), readings[...].astype(F32), noises[...].astype(F32),
-            jnp.ones((rows - members - 2, patch), F32),
+            sensors[...].astype(F32), readings[...].astype(F32)[None],
+            noises[...].astype(F32)[None], jnp.ones((rows - members - 2, patch), F32),
         ],
         axis=0,
     ).astype(BF16)
-
-    def peer(k):
-        other = lax.rem(me + space * n + k, peers)
-        return {"member": lax.rem(other, n), "space": other // n}
-
-    barrier = pltpu.get_barrier_semaphore()
-
-    def greet(k, carry):
-        pl.semaphore_signal(barrier, inc=1, device_id=peer(k), device_id_type=MESH)
-        return carry
-
-    lax.fori_loop(1, peers, greet, 0)
+    gathered[1, me] = pack[...]
 
     lane = lax.broadcasted_iota(jnp.int32, (obs_count, width), 1)
 
     def mark(group, carry):
         start = pl.multiple_of(group * 8, 8)
-        source = pl.multiple_of(me * domains + group * 8, 8)
-        columns = jnp.transpose(lists[pl.ds(source, 8), :] - me * domains)
+        columns = jnp.transpose(lists[pl.ds(start, 8), :] - me * domains)
         found = []
         for d in range(8):
             hit = columns[:, d : d + 1] == lane
@@ -95,26 +109,53 @@
 
     pl.semaphore_wait(barrier, peers - 1)
 
-    def side_copy(side, k):
+    def cross_copy(side):
         to_space = lax.rem(space + 1 - side + spaces, spaces)
         return pltpu.make_async_remote_copy(
-            pack, gathered.at[side, me], side_send.at[side, k], side_recv.at[side, k],
-            device_id={"member": partner(me, k, n), "space": to_space}, device_id_type=MESH,
-        )
+            pack, gathered.at[side, me], cross_send.at[side], cross_recv.at[side],
+            device_id={"space": to_space}, device_id_type=MESH,
+        )
+
+    def double_copies(side, step):
+        stride = n >> (step + 1)
+        to = partner(me, stride, n)
+        held = 1 << step
+        return [
+            pltpu.make_async_remote_copy(
+                gathered.at[side, lax.rem(me, 2 * stride) + j * 2 * stride],
+                gathered.at[side, lax.rem(me, 2 * stride) + j * 2 * stride],
+                side_send.at[side, held - 1 + j], side_recv.at[side, held - 1 + j],
+                device_id={"member": to}, device_id_type=MESH,
+            )
+            for j in range(held)
+        ]
+
+    def each_side(act):
+        act(1)
+
+        @pl.when(has_left)
+        def _():
+            act(0)
+
+        @pl.when(has_right)
+        def _():
+            act(2)
+
+    def begin(step):
+        return lambda side: [copy.start() for copy in double_copies(side, step)] and None
+
+    def finish(step):
+        return lambda side: [copy.wait() for copy in double_copies(side, step)] and None
 
     has_left, has_right = space > 0, space < spaces - 1
-    for k in range(1, n):
-        side_copy(1, k).start()
 
     @pl.when(has_right)
     def _():
-        for k in range(n):
-            side_copy(0, k).start()
+        cross_copy(0).start()
 
     @pl.when(has_left)
     def _():
-        for k in range(n):
-            side_copy(2, k).start()
+        cross_copy(2).start()
 
     def in_views(to, g):
         return (
@@ -142,7 +183,17 @@
         copy.start()
         own.append(copy)
 
-    gathered[1, me] = pack[...]
+    @pl.when(has_right)
+    def _():
+        cross_copy(0).wait_send()
+        cross_copy(2).wait_recv()
+
+    @pl.when(has_left)
+    def _():
+        cross_copy(2).wait_send()
+        cross_copy(0).wait_recv()
+
+    each_side(begin(0))
 
     @pl.when(space == 0)
     def _():
@@ -154,20 +205,10 @@
 
     lax.fori_loop(0, domains // 8, mark, 0)
 
-    for k in range(1, n):
-        side_copy(1, k).wait()
-
-    @pl.when(has_right)
-    def _():
-        for k in range(n):
-            side_copy(0, k).wait_send()
-            side_copy(2, k).wait_recv()
-
-    @pl.when(has_left)
-    def _():
-        for k in range(n):
-            side_copy(2, k).wait_send()
-            side_copy(0, k).wait_recv()
+    for step in range(n.bit_length() - 1):
+        if step:
+            each_side(begin(step))
+        each_side(finish(step))
 
     for side in range(3):
         for s in range(n):
@@ -191,7 +232,7 @@
     own_tier = lax.broadcasted_iota(jnp.int32, (domains, patch), 1) == (
         lax.broadcasted_iota(jnp.int32, (domains, patch), 0) + me * domains
     )
-    tier = jnp.sum(jnp.where(own_tier, tiers[...].astype(F32), 0.0), axis=1, keepdims=True)
+    tier = jnp.sum(jnp.where(own_tier, tiers[...].astype(F32)[None], 0.0), axis=1, keepdims=True)
     radius = (tier + 2.0) * (0.5 * obs_count)
     place = lax.broadcasted_iota(jnp.int32, (domains, width), 1)
     row = lax.broadcasted_iota(jnp.int32, (domains, width), 0)
@@ -200,7 +241,7 @@
     weights[...] = weight
     fit = jnp.sum(weight * (innov * innov))
     spread = jnp.sum(weight * squares)
-    first = lax.broadcasted_iota(jnp.int32, (8, LANES), 0) == 0
+    first = lax.broadcasted_iota(jnp.int32, (1, LANES), 1) == 0
     moved[...] = jnp.where(first, fit, spread)
 
     high, low = split(anomaly)
@@ -248,7 +289,7 @@
     lax.fori_loop(0, domains // 2, gram_group, 0)
 
     sums_all = lax.fori_loop(1, peers, end_sum, moved[...])
-    scale = sums_all[1:2, :] / sums_all[0:1, :]
+    scale = sums_all[:, 1:2] / sums_all[:, 0:1]
     eye = jnp.where(
         lax.broadcasted_iota(jnp.int32, (lines, LANES), 0)
         == lax.broadcasted_iota(jnp.int32, (lines, LANES), 1),
@@ -342,9 +383,15 @@
     return pl.pallas_call(
         functools.partial(analyse_kernel, n, spaces, halo, obs_count),
         out_shape=jax.ShapeDtypeStruct((members, patch, quantities), BF16),
-        in_specs=[anywhere] + [vmem] * 5,
+        in_specs=[anywhere] * 6,
         out_specs=vmem,
         scratch_shapes=[
+            pltpu.VMEM((members, patch), BF16),
+            pltpu.VMEM((patch,), BF16),
+            pltpu.VMEM((patch,), BF16),
+            pltpu.VMEM((domains, obs_count), jnp.int32),
+            pltpu.VMEM((patch,), jnp.int32),
+            dma((5,)),
             pltpu.VMEM((rows, patch), BF16),
             pltpu.VMEM((lines, domains, quantities), BF16),
             pltpu.VMEM((lines, domains, quantities), BF16),
@@ -357,16 +404,16 @@
             pltpu.VMEM((domains, lines, LANES), F32),
             pltpu.VMEM((domains, LANES), F32),
             pltpu.VMEM((domains, lines, LANES), BF16),
-            pltpu.VMEM((8, LANES), F32),
-            pltpu.VMEM((n * spaces, 8, LANES), F32),
+            pltpu.VMEM((1, LANES), F32),
+            pltpu.VMEM((n * spaces, 1, LANES), F32),
             dma((chunks, n)), dma((chunks, n)), dma((chunks, n)), dma((chunks, n)),
-            dma((2, chunks)), dma((3, n)), dma((3, n)), dma((n * spaces,)), dma((n * spaces,)),
+            dma((2, chunks)), dma((3,)), dma((3,)), dma((3, n)), dma((3, n)), dma((n * spaces,)), dma((n * spaces,)),
         ],
         compiler_params=pltpu.CompilerParams(
             collective_id=0, has_side_effects=True, vmem_limit_bytes=48 << 20
         ),
         name="analyse",
-    )(trials, sensors, readings[None], noises[None], lists, tiers[None])
+    )(trials, sensors, readings, noises, lists, tiers)
 
 
 def solution(mesh):

time: 104 us -> 107 us (1.029)
  Pallas kernels: 96.9 us -> 100 us
    pallas_call x1, Pallas kernels: 96.9 us -> 100 us  [per_device(): pl.pallas_call(functools.partial(analyse_kernel, n, spaces, halo, obs_cou...]
    broadcast_in_dim x3 -> x0, local copies, waits for them, and re-layouts: 2.05 us -> none  [the longest x1 0.68 us: per_device(): tiers[None]]
    unnamed x7 -> x13, local copies, waits for them, and re-layouts: 4.45 us -> 6.49 us
where the time goes in v3:
time: 107 us
  Pallas kernels  100 us (93%)
  local copies, waits for them, and re-layouts  6.49 us (6%)
    pallas_call x1, Pallas kernels, per_device(): pl.pallas_call(functools.partial(analyse_kernel, n, spaces, halo, obs_cou...  100 us
    unnamed x13, local copies, waits for them, and re-layouts  6.49 us

profile of v3, /device:TPU:13, one launch (start us, length us, event | category | flops | bytes accessed | tf_op | source)
XLA Modules:
  0.0 106.6 jit_solution(9518369676654995099)
XLA Ops:
  0.0 0.0 copy-start
  0.0 1.5 %copy-done = bf16[10,384,256]{2,1,0:T(8,128)(2,1)S(1)} copy-done((bf16[10,384,256]{2,1,0:T(8,128)(2,1)S(1)}, bf16[10,384,256]{2,1,0:T(8,128)(2,1)}, u32[]{:S(2)}) %copy-start) | copy-done | bytes 1966104
  1.5 0.0 copy-start.1
  1.5 0.9 copy-done.1
  2.5 0.0 copy-start.2
  2.5 0.7 copy-done.2
  3.2 0.0 copy-start.3
  3.2 0.7 copy-done.3
  3.9 0.0 copy-start.4
  3.9 0.7 copy-done.4
  4.5 0.0 copy-start.5
  4.5 0.7 copy-done.5
  5.2 100.1 %analyse.1 = bf16[10,384,256]{2,1,0:T(8,128)(2,1)S(1)} custom-call(bf16[10,384,256]{2,1,0:T(8,128)(2,1)S(1)} %copy-done, bf16[10,384]{1,0:T(8,128)(2,1)S(1)} %copy-done.2, bf16[384]{0:T(512)(128)(2,1)S(1)} %copy-done.4, bf16[384]{0:T(512)(128)(2,1)S(1)} %copy-done.5, s32[384,128]{1,0:T(8,128)S(1)} %copy-done.1, s32[384]{0:T(512)S(1)} %copy-done.3), custom_call_target="tpu_custom_call" | custom-call | tf_op jit(solution)/shard_map/analyse/pallas_call | solution.py:383
  105.4 1.3 %copy.8 = bf16[10,384,256]{2,1,0:T(8,128)(2,1)} copy(bf16[10,384,256]{2,1,0:T(8,128)(2,1)S(1)} %analyse.1) | data formatting | bytes 3932160
Async XLA Ops:
  0.0 1.5 %copy-start = (bf16[10,384,256]{2,1,0:T(8,128)(2,1)S(1)}, bf16[10,384,256]{2,1,0:T(8,128)(2,1)}, u32[]{:S(2)}) copy-start(bf16[10,384,256]{2,1,0:T(8,128)(2,1)} %x.1) | copy-start | bytes 5898244
  1.5 0.9 copy-start.1
  2.5 0.7 copy-start.2
  3.2 0.7 copy-start.3
  3.9 0.7 copy-start.4
  4.5 0.7 copy-start.5
